TPU v7x, 32 devices: a whole 2x2x4 slice. The times are simulated.
32 devices in a mesh: grp: 2 (over x), aux: 16 (over z, y, core).
Axes of the slice: x: 2, y: 2, z: 4, core: 2. Of those that a mesh axis runs over, the one named last changes fastest.
Arguments:
- three_index: bfloat16 [64, 256, 256], P('aux'), may hold values from -0.375 to 0.375
- relaxed: bfloat16 [512, 256], P('grp'), parts along dimension 0, may hold values from -0.375 to 0.375
- plus_amplitude: bfloat16 [512, 256], P('grp'), parts along dimension 0, may hold values from -0.375 to 0.375
- minus_amplitude: bfloat16 [512, 256], P('grp'), parts along dimension 0, may hold values from -0.375 to 0.375
- ground: bfloat16 [256, 256], replicated, may hold values from -0.375 to 0.375
- integral_grad: bfloat16 [3, 64, 512, 256], P(None, None, 'aux'), may hold values from -0.09375 to 0.09375
- metric_grad: bfloat16 [3, 64, 64], P(None, 'aux'), may hold values from -0.5 to 0.5
- function_atom: int32 [256], replicated, may hold values from 0 to 31, never falling along the last dimension, each value on 1 to 16 neighbouring positions
- aux_center: int32 [64], P('aux'), may hold values from 0 to 31, never falling along the last dimension, each value on 1 to 4 neighbouring positions
- block_list: int32 [512], replicated, may hold values from 0 to 255, as said below
- block_count: int32 [16], replicated, may hold values from 0 to 32, as said below
Outputs:
- gradient: float32 [3, 64], P(None, 'grp'), parts along dimension 1
There are 2 independent parts, one for each index of `grp`. A program takes and returns all parts, laid end to end along the dimension named above; an argument that names none is the same for every part. Nothing has to cross between parts.
Inputs may be any that keep to these rules, and one draw needn't show every extreme that they name: block_count[d] is the number of live slots of owner d; the counts sum to 256, and at least one owner has 32. `block_list`: slot s of owner d is entry d * 32 + s and is live when s < block_count[d]; each tile pair i * 16 + j is held by exactly one live slot; slots that are not live hold arbitrary tile pairs.
All inputs are finite; a program needn't handle non-finite values.
Results may differ from a plain program's by a relative error of at most 0.0032.
Values may be sent and summed in bfloat16 or wider, within the bound.
A program may use at most 64 MiB of HBM per device.

v0:
```python
import jax
import jax.numpy as jnp
from jax import lax
from jax.sharding import PartitionSpec as P

TILE = 16
NATOM = 32


def on_device(
    three_index,
    relaxed,
    plus_amplitude,
    minus_amplitude,
    ground,
    integral_grad,
    metric_grad,
    function_atom,
    aux_center,
    block_list,
    block_count,
):
    highest = lax.Precision.HIGHEST
    aux_local = three_index.shape[0]
    basis_count = three_index.shape[1]
    tile_count = basis_count // TILE
    slot_depth = integral_grad.shape[2]
    slot_total = block_list.shape[0]
    fitted = jnp.einsum("pab,ab->p", three_index, relaxed, preferred_element_type=jnp.float32)
    stacked = jnp.concatenate([plus_amplitude, minus_amplitude, ground], 0)
    halves = jnp.einsum(
        "ab,pbc->pac", stacked, three_index, preferred_element_type=jnp.float32
    ).astype(jnp.bfloat16)
    paired_half = halves[:, : 2 * basis_count].reshape(aux_local, 2, basis_count, basis_count)
    paired_half = jnp.concatenate([paired_half[:, 0], paired_half[:, 1]], axis=2)
    ground_half = halves[:, 2 * basis_count :]
    partners = jnp.concatenate([plus_amplitude, -minus_amplitude], axis=1)
    exchange_part = jnp.einsum(
        "pab,cb->pac", paired_half, partners, preferred_element_type=jnp.float32
    )
    crossed = jnp.einsum("pab,bc->pac", ground_half, relaxed, preferred_element_type=jnp.float32)
    triple = (
        fitted[:, None, None] * relaxed.astype(jnp.float32)[None]
        + exchange_part
        + crossed
        + jnp.swapaxes(crossed, 1, 2)
    )
    triple = triple.astype(jnp.bfloat16)
    blocked = triple.reshape(aux_local, tile_count, TILE, tile_count, TILE).transpose(0, 1, 3, 2, 4)
    blocked = blocked.reshape(aux_local, tile_count * tile_count, TILE * TILE)
    chosen = jnp.take(blocked, block_list, axis=1)
    slot_ids = jnp.arange(slot_total, dtype=jnp.int32)
    live_mask = (slot_ids % slot_depth < block_count[slot_ids // slot_depth]).astype(jnp.float32)
    arrived = lax.all_to_all(chosen, "aux", split_axis=1, concat_axis=0, tiled=True)
    first_slot = lax.axis_index("aux") * slot_depth
    tile_ids = lax.dynamic_slice_in_dim(block_list, first_slot, slot_depth)
    slot_mask = lax.dynamic_slice_in_dim(live_mask, first_slot, slot_depth)
    contracted = jnp.einsum(
        "pgf,kpgf->kgf", arrived, integral_grad, preferred_element_type=jnp.float32
    )
    slot_count = tile_ids.shape[0]
    row_sums = contracted.reshape(3, slot_count, TILE, TILE).sum(axis=3) * slot_mask[None, :, None]
    function_ids = (tile_ids // tile_count)[:, None] * TILE + jnp.arange(TILE, dtype=jnp.int32)[
        None, :
    ]
    atom_table = (
        function_atom[function_ids][:, :, None] == jnp.arange(NATOM, dtype=jnp.int32)[None, None, :]
    ).astype(jnp.float32)
    three_part = 2.0 * jnp.einsum("kgm,gma->ka", row_sums, atom_table, precision=highest)
    all_fitted = lax.all_gather(fitted, "aux", axis=0, tiled=True)
    coupling = jnp.einsum(
        "kpq,q->kp", metric_grad.astype(jnp.float32), all_fitted, precision=highest
    )
    aux_table = (aux_center[:, None] == jnp.arange(NATOM, dtype=jnp.int32)[None, :]).astype(
        jnp.float32
    )
    metric_part = jnp.einsum("kp,pa->ka", coupling * fitted[None, :], aux_table, precision=highest)
    return lax.psum(three_part - metric_part, "aux")


def solution(mesh):
    in_specs = (
        P("aux", None, None),
        P("grp", None),
        P("grp", None),
        P("grp", None),
        P(),
        P(None, None, "aux", None),
        P(None, "aux", None),
        P(),
        P("aux"),
        P(),
        P(),
    )
    out_specs = P(None, "grp")
    return jax.shard_map(
        on_device, mesh=mesh, in_specs=in_specs, out_specs=out_specs, check_vma=False
    )
```

profile of v0, /device:TPU:0, one launch (start us, length us, event | category | flops | bytes accessed | tf_op | source)
XLA Modules:
  0.0 119.7 jit_solution(17670021363365028496)
XLA Ops:
  0.0 0.0 copy-start
  0.0 1.8 %fusion = bf16[4,768,256]{2,1,0:T(8,128)(2,1)S(1)} fusion(bf16[4,256,256]{2,1,0:T(8,128)(2,1)} %param.11, bf16[256,256]{1,0:T(8,128)(2,1)} %param.15, bf16[256,256]{1,0:T(8,128)(2,1)} %param.14, bf16[256,256]{1,0:T(8,128)(2,1)} %param.13), kind=kOutput, calls=%fused_computation.5 | convolution fusion | flops 404619264 | bytes 2490368 | tf_op jit(solution)/shard_map/ab,pbc->pac/dot_general | solution.py:31
  1.9 0.0 copy-start.6
  1.9 0.0 copy-start.10
  1.9 0.1 slice.37
  2.0 0.0 copy-done.8
  2.0 0.3 fusion.8
  2.3 0.5 copy-done.6
  2.8 0.7 neg.3
  3.4 0.0 copy-done.10
  3.5 0.0 copy-start.4
  3.5 0.9 slice_bitcast_fusion.1
  4.3 0.3 copy.42
  4.7 0.0 copy-start.3
  4.7 0.0 copy-start.7
  4.7 0.0 copy-done.4
  4.7 1.9 %convolution_bitcast_fusion.1 = f32[4]{0:T(128)S(1)} fusion(bf16[4,256,256]{2,1,0:T(8,128)(2,1)S(1)} %copy-done.4, bf16[256,256,1]{1,0,2:T(8,128)(2,1)} %bitcast.80), kind=kOutput, calls=%fused_computation.13 | convolution fusion | flops 524288 | bytes 655376 | tf_op jit(solution)/shard_map/pab,ab->p/dot_general | solution.py:29
  6.6 0.5 copy-done.11
  7.1 0.0 copy-done.5
  7.1 0.0 copy-done.3
  7.1 0.0 copy-done.7
  7.1 0.5 fusion.3
  7.6 4.2 %reshape.108 = bf16[4,16,16,16,16]{4,3,2,1,0:T(8,128)(2,1)} reshape(bf16[4,256,256]{2,1,0:T(8,128)(2,1)S(1)} %fusion.3) | data formatting | bytes 1048576 | tf_op jit(solution)/shard_map/reshape | solution.py:49
  11.7 5.2 %copy.74 = bf16[4,16,16,16,16]{4,2,3,1,0:T(8,128)(2,1)} copy(bf16[4,16,16,16,16]{4,3,2,1,0:T(8,128)(2,1)} %reshape.108) | data formatting | bytes 1048576 | tf_op jit(solution)/shard_map/reshape | solution.py:49
  17.0 5.5 %reshape.109 = bf16[4,256,256]{2,1,0:T(8,128)(2,1)S(1)} reshape(bf16[4,16,16,16,16]{4,3,2,1,0:T(8,128)(2,1)} %bitcast.77) | data formatting | bytes 1048576 | tf_op jit(solution)/shard_map/reshape | solution.py:50
  22.5 0.4 copy.44
  22.9 2.4 %gather_fusion = bf16[512,4,256]{2,1,0:T(4,128)(2,1)S(1)} fusion(bf16[4,256,256]{2,0,1:T(4,128)(2,1)S(1)} %copy.44, s32[1024]{0:T(1024)S(1)} %pad_clamp_fusion.1), kind=kCustom, calls=%fused_computation | custom fusion | bytes 2099200 | tf_op jit(solution)/shard_map/jit(_take)/gather | solution.py:51
  25.3 0.0 copy-start.9
  25.3 0.0 copy-start.1
  25.3 2.7 %select_bitcast_fusion = bf16[4,512,256]{2,0,1:T(4,128)(2,1)} fusion(bf16[512,4,256]{2,1,0:T(4,128)(2,1)S(1)} %gather_fusion, pred[512]{0:T(512)(128)(4,1)S(1)} %compare_and_fusion), kind=kLoop, calls=%fused_computation.18 | loop fusion | flops 524288 | bytes 2097664 | tf_op jit(solution)/shard_map/jit(_take)/select_n | solution.py:51
  28.0 7.4 %all-to-all-start = ((bf16[4,512,256]{2,0,1:T(4,128)(2,1)}), bf16[4,512,256]{2,0,1:T(4,128)(2,1)S(1)}, u32[]{:S(2)}, u32[]{:S(2)}) async-start(bf16[4,512,256]{2,0,1:T(4,128)(2,1)} %select_bitcast_fusion), calls=%async_computation | async-start | bytes 2097152 | tf_op jit(solution)/shard_map/all_to_all | solution.py:54
  35.7 0.0 copy-done.9
  35.7 0.7 fusion.34
  36.5 4.3 %compare_select_fusion.2 = s32[512,1]{0,1:T(1,128)S(1)} fusion(s32[]{:T(128)} %bitcast.30, s32[]{:T(128)} %bitcast.31, s32[]{:T(128)} %bitcast.32, s32[]{:T(128)} %bitcast.33, s32[]{:T(128)} %bitcast.34, s32[]{:T(128)} %bitcast.36, s32[]{:T(128)} %bitcast.35), kind=kLoop, calls=%fused_computation.49 | loop fusion | flops 11776 | bytes 2076 | tf_op jit(solution)/shard_map/gather | solution.py:53
  40.8 5.7 %fusion.25 = f32[512]{0:T(512)S(1)} fusion(pred[512]{0:T(512)(128)(4,1)S(1)} %compare_reduce_fusion, pred[512]{0:T(512)(128)(4,1)S(1)} %compare_reduce_fusion.1, pred[512]{0:T(512)(128)(4,1)S(1)} %compare_reduce_fusion.2, pred[512]{0:T(512)(128)(4,1)S(1)} %compare_reduce_fusion.3, pred[512]{0:T(512)(128)(4,1)S(1)} %compare_reduce_fusion.4, ...), kind=kLoop, calls=%fused_computation.73 | loop fusion | flops 8704 | bytes 8740 | tf_op jit(solution)/shard_map/convert_element_type | solution.py:53
  46.4 0.1 dynamic_slice.6
  46.5 0.1 fusion.28
  46.6 0.1 compare_select_fusion
  46.7 0.1 reshape.144
  46.8 0.0 copy-done.1
  46.8 0.0 copy-start.14
  46.8 0.0 copy-start.12
  46.8 3.5 %gather_fusion.1 = s32[512]{0:T(512)S(1)} fusion(s32[256]{0:T(256)S(1)} %copy-done.1, s32[1024]{0:T(1024)S(1)} %pad_clamp_fusion), kind=kCustom, calls=%fused_computation.1 | custom fusion | bytes 6144 | tf_op jit(solution)/shard_map/gather | solution.py:67
  50.3 0.1 reshape.143
  50.4 0.1 copy.46
  50.5 0.0 copy-done.14
  50.5 0.6 dynamic-slice
  51.7 0.0 copy-done.12
  51.7 0.2 dynamic-update-slice
  52.0 33.9 %all-reduce = f32[64]{0:T(128)S(1)} all-reduce(f32[64]{0:T(128)S(1)} %dynamic-update-slice), channel_id=1, replica_groups=mesh['grp'=2,'aux'=16] {'aux'}, use_global_device_ids=true, to_apply=%add | all-reduce | flops 64 | bytes 512
  85.9 0.0 copy-done
  85.9 0.1 fusion.29
  86.0 0.0 all-to-all-done
  86.1 0.2 copy.59
  86.3 0.0 copy-start.2
  86.3 0.3 bitcast_convert_fusion
  86.6 1.5 %copy-done.2 = bf16[3,64,32,256]{3,2,1,0:T(8,128)(2,1)S(1)} copy-done((bf16[3,64,32,256]{3,2,1,0:T(8,128)(2,1)S(1)}, bf16[3,64,32,256]{3,2,1,0:T(8,128)(2,1)}, u32[]{:S(2)}) %copy-start.2) | copy-done | bytes 3145752
  88.2 0.7 multiply_reduce_fusion
  88.9 0.2 copy.57
  89.1 0.1 bitcast_reduce_fusion
  89.2 0.3 fusion.4
  89.5 0.0 copy-done.13
  89.5 0.2 convolution_subtract_fusion
  89.7 30.1 %psum.7 = f32[3,32]{1,0:T(4,128)} all-reduce(f32[3,32]{1,0:T(4,128)S(1)} %convolution_subtract_fusion), channel_id=1, replica_groups=mesh['grp'=2,'aux'=16] {'aux'}, use_global_device_ids=true, to_apply=%region_1.2 | all-reduce | flops 96 | bytes 768 | tf_op jit(solution)/shard_map/psum | solution.py:78
  (20 shorter events, 0.4 us)
Async XLA Ops:
  0.0 85.9 %copy-start = (bf16[3,4,64]{2,1,0:T(4,128)(2,1)S(1)}, bf16[3,4,64]{2,1,0:T(4,128)(2,1)}, u32[]{:S(2)}) copy-start(bf16[3,4,64]{2,1,0:T(4,128)(2,1)} %param.17) | copy-start | bytes 4612
  0.0 2.0 %copy-start.8 = (bf16[256,256]{1,0:T(8,128)(2,1)S(1)}, bf16[256,256]{1,0:T(8,128)(2,1)}, u32[]{:S(2)}) copy-start(bf16[256,256]{1,0:T(8,128)(2,1)} %param.12) | copy-start | bytes 393220
  1.9 0.9 copy-start.6
  1.9 1.6 %copy-start.10 = (s32[512]{0:T(512)S(1)}, s32[512]{0:T(512)}, u32[]{:S(2)}) copy-start(s32[512]{0:T(512)} %param.20) | copy-start | bytes 6148
  3.5 1.2 %copy-start.4 = (bf16[4,256,256]{2,1,0:T(8,128)(2,1)S(1)}, bf16[4,256,256]{2,1,0:T(8,128)(2,1)}, u32[]{:S(2)}) copy-start(bf16[4,256,256]{2,1,0:T(8,128)(2,1)} %param.11) | copy-start | bytes 1572868
  4.3 2.8 %copy-start.5 = (bf16[256,256]{1,0:T(8,128)(2,1)S(1)}, bf16[256,256]{1,0:T(8,128)(2,1)}, u32[]{:S(2)}) copy-start(bf16[256,256]{1,0:T(8,128)(2,1)} %param.13) | copy-start | bytes 393220
  4.7 2.4 %copy-start.3 = (bf16[4,256,256]{2,1,0:T(8,128)(2,1)S(1)}, bf16[4,256,256]{2,1,0:T(8,128)(2,1)}, u32[]{:S(2)}) copy-start(bf16[4,256,256]{2,1,0:T(8,128)(2,1)} %get-tuple-element.6) | copy-start | bytes 1572868
  4.7 2.4 %copy-start.7 = (bf16[256,256]{1,0:T(8,128)(2,1)S(1)}, bf16[256,256]{1,0:T(8,128)(2,1)}, u32[]{:S(2)}) copy-start(bf16[256,256]{1,0:T(8,128)(2,1)} %neg.3) | copy-start | bytes 393220
  6.6 0.5 copy-start.11
  25.3 10.4 %copy-start.9 = (s32[16]{0:T(128)S(1)}, s32[16]{0:T(128)}, u32[]{:S(2)}) copy-start(s32[16]{0:T(128)} %param.21) | copy-start | bytes 196
  25.3 21.4 %copy-start.1 = (s32[256]{0:T(256)S(1)}, s32[256]{0:T(256)}, u32[]{:S(2)}) copy-start(s32[256]{0:T(256)} %param.18) | copy-start | bytes 3076
  28.0 58.0 %all-to-all-start = ((bf16[4,512,256]{2,0,1:T(4,128)(2,1)}), bf16[4,512,256]{2,0,1:T(4,128)(2,1)S(1)}, u32[]{:S(2)}, u32[]{:S(2)}) async-start(bf16[4,512,256]{2,0,1:T(4,128)(2,1)} %select_bitcast_fusion), calls=%async_computation | async-start | bytes 2097152 | tf_op jit(solution)/shard_map/all_to_all | solution.py:54
  46.8 3.7 %copy-start.14 = (u32[32]{0:T(128)S(1)}, u32[32]{0:T(128)}, u32[]{:S(2)}) copy-start(u32[32]{0:T(128)} %constant.97) | copy-start | bytes 388
  46.8 4.9 %copy-start.12 = (f32[4]{0:T(128)S(1)}, f32[4]{0:T(128)}, u32[]{:S(2)}) copy-start(f32[4]{0:T(128)} %copy-done.11) | copy-start | bytes 52
  86.3 1.9 %copy-start.2 = (bf16[3,64,32,256]{3,2,1,0:T(8,128)(2,1)S(1)}, bf16[3,64,32,256]{3,2,1,0:T(8,128)(2,1)}, u32[]{:S(2)}) copy-start(bf16[3,64,32,256]{3,2,1,0:T(8,128)(2,1)} %param.16) | copy-start | bytes 9437188
  88.2 1.3 %copy-start.13 = (s32[4]{0:T(128)S(1)}, s32[4]{0:T(128)}, u32[]{:S(2)}) copy-start(s32[4]{0:T(128)} %param.19) | copy-start | bytes 52
where the time goes:
time: 120 us
  blocking collectives  64 us (53%)
  local copies, waits for them, and re-layouts  27.3 us (23%)
  other arithmetic  15 us (12%)
  starting transfers between devices  7.41 us (6%)
  matrix products  5.13 us (4%)
    unnamed x1, blocking collectives  33.9 us
    psum x1, blocking collectives, on_device(): return lax.psum(three_part - metric_part, 'aux')  30.1 us
    reshape x2, local copies, waits for them, and re-layouts, on_device(): triple.reshape(aux_local, tile_count, TILE, tile_count, TILE)  9.39 us
    all_to_all x1, starting transfers between devices, on_device(): lax.all_to_all(chosen, 'aux', split_axis=1, concat_axis=0, tiled=True)  7.41 us
    reshape x2, local copies, waits for them, and re-layouts, on_device(): blocked = blocked.reshape(aux_local, tile_count * tile_count, TILE * TILE)  5.89 us
    convert_element_type x1, other arithmetic, on_device(): (slot_ids % slot_depth < block_count[slot_ids // slot_depth]).astype(jnp....  5.67 us
    gather x10, other arithmetic, on_device(): block_count[slot_ids // slot_depth]  4.61 us
    gather x3, local copies, waits for them, and re-layouts, on_device(): function_atom[function_ids][:, :, None]  3.67 us
  transfers between devices with their start and end apart: 1, of which 0 were waited for; matrix products, arithmetic and copies ran while one was open for 13% of the time, Pallas kernels for 0%

commit v1 on v0

v1 whole, which is shorter than its diff:
```python
import functools

import jax
import jax.numpy as jnp
from jax import lax
from jax.experimental import pallas as pl
from jax.experimental.pallas import tpu as pltpu
from jax.sharding import PartitionSpec as P

TILE = 16
NATOM = 32
F32 = jnp.float32
BF16 = jnp.bfloat16
MESH = pl.DeviceIdType.MESH


def iota(shape, axis):
    return lax.broadcasted_iota(jnp.int32, shape, axis)


def dot(a, b, ca=1, cb=0):
    return lax.dot_general(a, b, (((ca,), (cb,)), ((), ())), preferred_element_type=F32)


def swap_tiles(x):
    quads = x.reshape(TILE, 2, 8, 256)
    rows = []
    for high_v in range(2):
        lanes = []
        for high_i in range(2):
            z = quads[:, high_i, :, high_v * 128 : high_v * 128 + 128]
            z = z.reshape(TILE * 8, 128)
            sub = iota(z.shape, 0)
            lane = iota(z.shape, 1) // TILE
            for s in (4, 2, 1):
                bit_i = (sub // s) % 2
                bit_v = (lane // s) % 2
                down = pltpu.roll(z, z.shape[0] - s, 0)
                down = pltpu.roll(down, TILE * s, 1)
                up = pltpu.roll(z, s, 0)
                up = pltpu.roll(up, 128 - TILE * s, 1)
                z = jnp.where(bit_i == bit_v, z, jnp.where(bit_i == 0, down, up))
            lanes.append(z.reshape(TILE, 1, 8, 128))
        rows.append(jnp.concatenate(lanes, axis=3))
    return jnp.concatenate(rows, axis=1).reshape(256, 256)


def density_kernel(
    owners, b_ref, relaxed_ref, plus_ref, minus_ref, ground_ref, list_ref, chosen_ref, fit_ref
):
    aux_local = b_ref.shape[0]
    slots = list_ref.shape[0]
    me = lax.axis_index("aux")
    relaxed = relaxed_ref[...]
    a = iota((256, 256), 0)
    b = iota((256, 256), 1)
    perm = ((a % TILE) * TILE + a // TILE == b).astype(BF16)
    plus = dot(perm, plus_ref[...]).astype(BF16)
    minus = dot(perm, minus_ref[...]).astype(BF16)
    ground = dot(perm, ground_ref[...]).astype(BF16)
    relaxed_cols = dot(relaxed, perm, 1, 1).astype(BF16)
    relaxed_turned = dot(perm, relaxed, 1, 1).astype(BF16)
    relaxed_both = dot(perm, relaxed_cols)
    picked = (list_ref[...] == iota((slots, 256), 1)).astype(BF16)
    lane = iota(fit_ref.shape, 1)
    fit_row = jnp.zeros(fit_ref.shape, F32)
    for p in range(aux_local):
        slab = b_ref[p]
        fitted = jnp.sum(slab.astype(F32) * relaxed.astype(F32), axis=0, keepdims=True)
        fitted = jnp.sum(fitted, axis=1, keepdims=True)
        fit_row = jnp.where(lane == me * aux_local + p, fitted, fit_row)
        plus_half = dot(plus, slab).astype(BF16)
        minus_half = dot(minus, slab).astype(BF16)
        ground_half = dot(ground, slab).astype(BF16)
        triple = (
            fitted * relaxed_both
            + dot(plus_half, plus, 1, 1)
            - dot(minus_half, minus, 1, 1)
            + dot(ground_half, relaxed_cols)
            + dot(relaxed_turned, ground_half, 1, 1)
        )
        blocked = swap_tiles(triple.astype(BF16).astype(F32)).astype(BF16)
        chosen = dot(picked, blocked, 1, 1)
        chosen_ref[:, p] = chosen.reshape(owners, slots // owners, 256).astype(BF16)
    fit_ref[...] = fit_row


def exchange_kernel(
    n,
    count_ref,
    center_ref,
    chosen_ref,
    fit_ref,
    metric_ref,
    list_ref,
    atom_ref,
    integral_ref,
    out_ref,
    integral,
    arrived,
    fits,
    parts,
    load_sems,
    send_sems,
    recv_sems,
    fit_send,
    fit_recv,
    part_send,
    part_recv,
):
    me = lax.axis_index("aux")
    depth = integral.shape[2]
    aux_local = arrived.shape[1]

    loads = [
        pltpu.make_async_copy(integral_ref.at[c], integral.at[c], load_sems.at[c]) for c in range(3)
    ]
    loads.append(pltpu.make_async_copy(chosen_ref.at[me], arrived.at[me], load_sems.at[3]))
    loads.append(pltpu.make_async_copy(fit_ref, fits.at[me], load_sems.at[4]))
    for load in loads:
        load.start()

    barrier = pltpu.get_barrier_semaphore()

    def peer_of(k):
        return lax.rem(me + k, n)

    def greet(k, c):
        pl.semaphore_signal(barrier, inc=1, device_id={"aux": peer_of(k)}, device_id_type=MESH)
        return c

    lax.fori_loop(1, n, greet, 0)
    pl.semaphore_wait(barrier, n - 1)

    def tiles_to(peer, slot):
        return pltpu.make_async_remote_copy(
            src_ref=chosen_ref.at[peer],
            dst_ref=arrived.at[slot],
            send_sem=send_sems.at[peer],
            recv_sem=recv_sems.at[slot],
            device_id={"aux": peer},
            device_id_type=MESH,
        )

    def fit_to(peer, slot):
        return pltpu.make_async_remote_copy(
            src_ref=fit_ref,
            dst_ref=fits.at[slot],
            send_sem=fit_send.at[peer],
            recv_sem=fit_recv.at[slot],
            device_id={"aux": peer},
            device_id_type=MESH,
        )

    def part_to(peer, slot):
        return pltpu.make_async_remote_copy(
            src_ref=parts.at[me],
            dst_ref=parts.at[slot],
            send_sem=part_send.at[peer],
            recv_sem=part_recv.at[slot],
            device_id={"aux": peer},
            device_id_type=MESH,
        )

    def launch(k, c):
        fit_to(peer_of(k), me).start()
        tiles_to(peer_of(k), me).start()
        return c

    lax.fori_loop(1, n, launch, 0)

    a = iota((TILE, 256), 0)
    b = iota((TILE, 256), 1)
    atoms = jnp.where(b // TILE == a, atom_ref[...].astype(F32), 0.0).astype(BF16)
    spread = (iota((256, 256), 0) % TILE == iota((256, 256), 1) // TILE).astype(BF16)
    atoms = dot(atoms, spread).astype(BF16)
    own_list = list_ref[pl.ds(me * depth, depth), :]
    in_row = (own_list // TILE == iota((depth, TILE), 1)).astype(BF16)
    slot_atoms = dot(in_row, atoms)
    live = iota((depth, 256), 0) < count_ref[me]
    slot_atoms = jnp.where(live, slot_atoms, -1.0).astype(jnp.int32)

    for load in loads:
        load.wait()

    def take(src, sums):
        for p in range(aux_local):
            tile = arrived[src, p].astype(F32)
            row = src * aux_local + p
            sums = tuple(
                total + tile * integral[c, row].astype(F32) for c, total in enumerate(sums)
            )
        return sums

    sums = take(me, tuple(jnp.zeros((depth, 256), F32) for _ in range(3)))
    all_fits = fits[me]

    def arrive(k, carry):
        sums, total_fits = carry
        src = lax.rem(me + n - k, n)
        fit_to(src, src).wait_recv()
        total_fits = total_fits + fits[src]
        tiles_to(src, src).wait_recv()
        return take(src, sums), total_fits

    own_fits = all_fits
    sums, all_fits = lax.fori_loop(1, n, arrive, (sums, all_fits))

    lane = iota((1, 128), 1)
    rows = iota((aux_local, all_fits.shape[1]), 0)
    lanes = iota((aux_local, all_fits.shape[1]), 1)
    fit_column = jnp.sum(
        jnp.where(lanes == me * aux_local + rows, own_fits[:1], 0.0), axis=1, keepdims=True
    )
    table = jnp.zeros((aux_local, 128), F32)
    for p in range(aux_local):
        hit = (iota((aux_local, 128), 0) == p) & (iota((aux_local, 128), 1) == center_ref[p])
        table = jnp.where(hit, fit_column, table)
    width = metric_ref.shape[2]
    out_rows = []
    for c in range(3):
        coupling = jnp.sum(
            metric_ref[c].astype(F32) * all_fits[:1, :width], axis=1, keepdims=True
        )
        metric_part = jnp.sum(coupling * table, axis=0, keepdims=True)
        row = -metric_part
        for atom in range(NATOM):
            hit = jnp.where(slot_atoms == atom, sums[c], 0.0)
            hit = jnp.sum(hit, axis=0, keepdims=True)
            hit = jnp.sum(hit, axis=1, keepdims=True)
            row = row + jnp.where(lane == atom, 2.0 * hit, 0.0)
        out_rows.append(row)
    mine = jnp.concatenate(out_rows + [jnp.zeros((5, 128), F32)], axis=0)
    parts[me] = mine

    def send_part(k, c):
        part_to(peer_of(k), me).start()
        return c

    lax.fori_loop(1, n, send_part, 0)

    def take_part(k, total):
        src = lax.rem(me + n - k, n)
        part_to(src, src).wait_recv()
        return total

    lax.fori_loop(1, n, take_part, 0)
    total = jnp.sum(parts[...], axis=0)
    out_ref[...] = total[:3, :NATOM]

    def drain(k, c):
        peer = peer_of(k)
        fit_to(peer, me).wait_send()
        tiles_to(peer, me).wait_send()
        part_to(peer, me).wait_send()
        return c

    lax.fori_loop(1, n, drain, 0)


def on_device(
    n,
    three_index,
    relaxed,
    plus_amplitude,
    minus_amplitude,
    ground,
    integral_grad,
    metric_grad,
    function_atom,
    aux_center,
    block_list,
    block_count,
):
    aux_local = three_index.shape[0]
    slots = block_list.shape[0]
    aux_total, depth, width = integral_grad.shape[1:]
    fit_lanes = -(-aux_total // 128) * 128
    column = block_list.reshape(slots, 1)
    vmem = pl.BlockSpec(memory_space=pltpu.VMEM)
    smem = pl.BlockSpec(memory_space=pltpu.SMEM)
    anywhere = pl.BlockSpec(memory_space=pl.ANY)
    chosen, fit = pl.pallas_call(
        functools.partial(density_kernel, n),
        out_shape=(
            jax.ShapeDtypeStruct((n, aux_local, depth, width), BF16),
            jax.ShapeDtypeStruct((8, fit_lanes), F32),
        ),
        in_specs=[vmem] * 6,
        out_specs=(vmem, vmem),
        name="density",
    )(three_index, relaxed, plus_amplitude, minus_amplitude, ground, column)
    return pl.pallas_call(
        functools.partial(exchange_kernel, n),
        out_shape=jax.ShapeDtypeStruct((3, NATOM), F32),
        in_specs=[smem, smem, anywhere, anywhere, vmem, vmem, vmem, anywhere],
        out_specs=vmem,
        scratch_shapes=[
            pltpu.VMEM((3, aux_total, depth, width), BF16),
            pltpu.VMEM((n, aux_local, depth, width), BF16),
            pltpu.VMEM((n, 8, fit_lanes), F32),
            pltpu.VMEM((n, 8, 128), F32),
            pltpu.SemaphoreType.DMA((5,)),
            pltpu.SemaphoreType.DMA((n,)),
            pltpu.SemaphoreType.DMA((n,)),
            pltpu.SemaphoreType.DMA((n,)),
            pltpu.SemaphoreType.DMA((n,)),
            pltpu.SemaphoreType.DMA((n,)),
            pltpu.SemaphoreType.DMA((n,)),
        ],
        compiler_params=pltpu.CompilerParams(collective_id=0, has_side_effects=True),
        name="exchange",
    )(
        block_count,
        aux_center,
        chosen,
        fit,
        metric_grad,
        column,
        function_atom.reshape(1, -1),
        integral_grad,
    )


def solution(mesh):
    in_specs = (
        P("aux", None, None),
        P("grp", None),
        P("grp", None),
        P("grp", None),
        P(),
        P(None, None, "aux", None),
        P(None, "aux", None),
        P(),
        P("aux"),
        P(),
        P(),
    )
    out_specs = P(None, "grp")
    return jax.shard_map(
        functools.partial(on_device, mesh.shape["aux"]),
        mesh=mesh,
        in_specs=in_specs,
        out_specs=out_specs,
        check_vma=False,
    )
```

time: 120 us -> 49.9 us (0.42)
  blocking collectives: 64 us -> 0 us
  Pallas kernels: 0 us -> 46.9 us
  local copies, waits for them, and re-layouts: 27.3 us -> 2.79 us
  other arithmetic: 15 us -> 0 us
  starting transfers between devices: 7.41 us -> 0 us
  matrix products: 5.13 us -> 0 us
    pallas_call x0 -> x2, Pallas kernels: none -> 46.9 us  [the longest x1 40.4 us: on_device(): pl.pallas_call(functools.partial(exchange_kernel, n), out_shape=jax.Shape...]
    unnamed x1 -> x0, blocking collectives: 33.9 us -> none
    psum x1 -> x0, blocking collectives: 30.1 us -> none  [on_device(): return lax.psum(three_part - metric_part, 'aux')]
    reshape x4 -> x1, local copies, waits for them, and re-layouts: 15.3 us -> 1.54 us  [on_device(): column = block_list.reshape(slots, 1)]
    all_to_all x1 -> x0, starting transfers between devices: 7.41 us -> none  [on_device(): lax.all_to_all(chosen, 'aux', split_axis=1, concat_axis=0, tiled=True)]
    gather x5 -> x0, local copies, waits for them, and re-layouts: 6.78 us -> none  [the longest x3 3.67 us: on_device(): function_atom[function_ids][:, :, None]]
    convert_element_type x2 -> x0, other arithmetic: 5.69 us -> none  [the longest x1 5.67 us: on_device(): (slot_ids % slot_depth < block_count[slot_ids // slot_depth]).astype(jnp....]
    dot_general x7 -> x0, matrix products: 5.13 us -> none  [the longest x1 1.91 us: on_device(): jnp.einsum('pab,ab->p', three_index, relaxed, preferred_element_type=jnp....]
  transfers between devices with their start and end apart: 1 -> 0, of which waited for: 0 -> 0; matrix products, arithmetic and copies ran while one was open for 13% -> 0% of each run, Pallas kernels for 0% -> 0%
where the time goes in v1:
time: 49.9 us; the launch traced here: 49.7 us
  Pallas kernels  46.9 us (94%)
  local copies, waits for them, and re-layouts  2.79 us (6%)
    pallas_call x1, Pallas kernels, on_device(): pl.pallas_call(functools.partial(exchange_kernel, n), out_shape=jax.Shape...  40.4 us
    pallas_call x1, Pallas kernels, on_device(): pl.pallas_call(functools.partial(density_kernel, n), out_shape=(jax.Shape...  6.48 us
    reshape x1, local copies, waits for them, and re-layouts, on_device(): column = block_list.reshape(slots, 1)  1.54 us
    unnamed x1, local copies, waits for them, and re-layouts  1.25 us

profile of v1, /device:TPU:0, one launch (start us, length us, event | category | flops | bytes accessed | tf_op | source)
XLA Modules:
  0.0 49.7 jit_solution(1850546543212470971)
XLA Ops:
  0.0 1.5 %copy.12.list_ref = s32[512,1]{1,0:T(8,128)} copy(s32[512,1]{0,1:T(1,128)} %bitcast.2) | data formatting | bytes 4096 | tf_op jit(solution)/shard_map/reshape | solution.py:279
  1.5 6.5 %density.1 = (bf16[16,4,32,256]{3,2,1,0:T(8,128)(2,1)}, f32[8,128]{1,0:T(8,128)}) custom-call(bf16[4,256,256]{2,1,0:T(8,128)(2,1)} %b_ref.1, bf16[256,256]{1,0:T(8,128)(2,1)} %relaxed_ref.1, bf16[256,256]{1,0:T(8,128)(2,1)} %plus_ref.1, bf16[256,256]{1,0:T(8,128)(2,1)} %minus_ref.1, bf16[256,256]{1,0:T(8,128)(2,1)} %ground_ref.1, s32[512,1]{1,0:T(8,128)} %copy.12.list_ref), custom_call_target="tpu_custom_call" | custom-call | tf_op jit(solution)/shard_map/density/pallas_call | solution.py:283
  8.0 40.4 %exchange.1 = f32[3,32]{1,0:T(4,128)} custom-call(s32[16]{0:T(128)} %count_ref.1, s32[4]{0:T(128)} %center_ref.1, bf16[16,4,32,256]{3,2,1,0:T(8,128)(2,1)} %get-tuple-element.7.chosen_ref, f32[8,128]{1,0:T(8,128)} %get-tuple-element.8.fit_ref, bf16[3,4,64]{2,1,0:T(4,128)(2,1)} %metric_ref.1, s32[512,1]{1,0:T(8,128)} %copy.12.list_ref, s32[1,256]{1,0:T(1,128)} %bitcast.3, ...), custom_call_target="tpu_custom_call" | custom-call | tf_op jit(solution)/shard_map/exchange/pallas_call | solution.py:293
  48.5 1.3 %copy.15 = f32[3,32]{1,0:T(4,128)} copy(f32[3,32]{1,0:T(4,128)} %exchange.1) | data formatting | bytes 768

commit v2 on v1

v2 whole, which is shorter than its diff:
```python
import functools

import jax
import jax.numpy as jnp
from jax import lax
from jax.experimental import pallas as pl
from jax.experimental.pallas import tpu as pltpu
from jax.sharding import PartitionSpec as P

TILE = 16
NATOM = 32
F32 = jnp.float32
BF16 = jnp.bfloat16
MESH = pl.DeviceIdType.MESH


def iota(shape, axis):
    return lax.broadcasted_iota(jnp.int32, shape, axis)


def dot(a, b, ca=1, cb=0):
    return lax.dot_general(a, b, (((ca,), (cb,)), ((), ())), preferred_element_type=F32)


def swap_tiles(x):
    quads = x.reshape(TILE, 2, 8, 256)
    rows = []
    for high_v in range(2):
        lanes = []
        for high_i in range(2):
            z = quads[:, high_i, :, high_v * 128 : high_v * 128 + 128]
            z = z.reshape(TILE * 8, 128)
            sub = iota(z.shape, 0)
            lane = iota(z.shape, 1) // TILE
            for s in (4, 2, 1):
                bit_i = (sub // s) % 2
                bit_v = (lane // s) % 2
                down = pltpu.roll(z, z.shape[0] - s, 0)
                down = pltpu.roll(down, TILE * s, 1)
                up = pltpu.roll(z, s, 0)
                up = pltpu.roll(up, 128 - TILE * s, 1)
                z = jnp.where(bit_i == bit_v, z, jnp.where(bit_i == 0, down, up))
            lanes.append(z.reshape(TILE, 1, 8, 128))
        rows.append(jnp.concatenate(lanes, axis=3))
    return jnp.concatenate(rows, axis=1).reshape(256, 256)


def split3(x):
    high = x.astype(BF16)
    rest = x - high.astype(F32)
    middle = rest.astype(BF16)
    low = (rest - middle.astype(F32)).astype(BF16)
    return high, middle, low


def select_dot(x, table):
    rows = x.shape[0]
    terms = dot(jnp.concatenate([t.astype(F32) for t in split3(x)], axis=0).astype(BF16), table)
    return terms[:rows] + terms[rows : 2 * rows] + terms[2 * rows :]


def gradient_kernel(
    n,
    groups,
    count_ref,
    center_ref,
    b_ref,
    relaxed_ref,
    plus_ref,
    minus_ref,
    ground_ref,
    metric_ref,
    list_ref,
    atom_ref,
    integral_ref,
    out_ref,
    integral,
    foreign,
    chosen,
    arrived,
    fits,
    parts,
    load_sems,
    far_send,
    far_recv,
    near_send,
    near_recv,
    send_sems,
    recv_sems,
    fit_send,
    fit_recv,
    part_send,
    part_recv,
):
    me = lax.axis_index("aux")
    group = lax.axis_index("grp")
    half = n // 2
    depth = integral.shape[2]
    aux_local = b_ref.shape[0]
    share = aux_local // groups
    slots = list_ref.shape[1]
    side = me // half
    spot = me % half
    base = side * half
    other_base = (1 - side) * half
    counterpart = other_base + spot

    loads = [
        pltpu.make_async_copy(integral_ref.at[c], integral.at[c], load_sems.at[c]) for c in range(3)
    ]
    for load in loads:
        load.start()

    barrier = pltpu.get_barrier_semaphore()

    def xor(a, k):
        value, bit = me - me, 1
        while bit < n:
            value = value + ((a // bit) % 2 + (k // bit) % 2) % 2 * bit
            bit *= 2
        return value

    def greet(k, c):
        pl.semaphore_signal(barrier, inc=1, device_id={"aux": xor(me, k)}, device_id_type=MESH)
        return c

    lax.fori_loop(1, n, greet, 0)
    for d in range(1, groups):
        pl.semaphore_signal(
            barrier, inc=1, device_id={"grp": lax.rem(group + d, groups)}, device_id_type=MESH
        )

    def far(q):
        p = group * share + q
        return pltpu.make_async_remote_copy(
            src_ref=b_ref.at[p],
            dst_ref=foreign.at[p],
            send_sem=far_send.at[q],
            recv_sem=far_recv.at[q],
            device_id={"aux": counterpart},
            device_id_type=MESH,
        )

    def near(d, q, source):
        p = source * share + q
        return pltpu.make_async_remote_copy(
            src_ref=foreign.at[p],
            dst_ref=foreign.at[p],
            send_sem=near_send.at[d - 1, q],
            recv_sem=near_recv.at[d - 1, q],
            device_id={"grp": lax.rem(group + d, groups)},
            device_id_type=MESH,
        )

    def tiles(p, peer, slot):
        return pltpu.make_async_remote_copy(
            src_ref=chosen.at[peer, p],
            dst_ref=arrived.at[slot, p],
            send_sem=send_sems.at[p, peer],
            recv_sem=recv_sems.at[p, slot],
            device_id={"aux": base + peer},
            device_id_type=MESH,
        )

    def fit_to(peer, slot):
        return pltpu.make_async_remote_copy(
            src_ref=fits.at[spot],
            dst_ref=fits.at[slot],
            send_sem=fit_send.at[peer],
            recv_sem=fit_recv.at[slot],
            device_id={"aux": base + peer},
            device_id_type=MESH,
        )

    def part_to(peer, slot):
        return pltpu.make_async_remote_copy(
            src_ref=parts.at[me],
            dst_ref=parts.at[slot],
            send_sem=part_send.at[peer],
            recv_sem=part_recv.at[slot],
            device_id={"aux": peer},
            device_id_type=MESH,
        )

    pl.semaphore_wait(barrier, n - 1 + groups - 1)
    for q in range(share):
        far(q).start()

    relaxed = relaxed_ref[...]
    a = iota((256, 256), 0)
    b = iota((256, 256), 1)
    perm = ((a % TILE) * TILE + a // TILE == b).astype(BF16)
    plus = dot(perm, plus_ref[...]).astype(BF16)
    minus = dot(perm, minus_ref[...]).astype(BF16)
    ground = dot(perm, ground_ref[...]).astype(BF16)
    relaxed_cols = dot(relaxed, perm, 1, 1).astype(BF16)
    relaxed_turned = dot(perm, relaxed, 1, 1).astype(BF16)
    relaxed_both = dot(perm, relaxed_cols)
    relaxed_wide = relaxed.astype(F32)
    half_slots = slots // 2
    listed = list_ref[...]
    listed = jnp.where(side == 0, listed[:, :half_slots], listed[:, half_slots:])
    picked = (listed == iota((256, half_slots), 0)).astype(F32).T.astype(BF16)
    fit_lane = iota(fits.shape[1:], 1)

    def density(slab, p, owner, fit_row):
        fitted = jnp.sum(slab.astype(F32) * relaxed_wide, axis=0, keepdims=True)
        fitted = jnp.sum(fitted, axis=1, keepdims=True)
        plus_half = dot(plus, slab).astype(BF16)
        minus_half = dot(minus, slab).astype(BF16)
        ground_half = dot(ground, slab).astype(BF16)
        triple = (
            fitted * relaxed_both
            + dot(plus_half, plus, 1, 1)
            - dot(minus_half, minus, 1, 1)
            + dot(ground_half, relaxed_cols)
            + dot(relaxed_turned, ground_half, 1, 1)
        )
        blocked = swap_tiles(triple.astype(BF16).astype(F32)).astype(BF16)
        tile_rows = dot(picked, blocked, 1, 1)
        chosen[:, p] = tile_rows.reshape(half, depth, 256).astype(BF16)

        def send(k, c):
            peer = xor(spot, half - k)
            tiles(p, peer, spot).start()
            return c

        lax.fori_loop(1, half, send, 0)
        return jnp.where(fit_lane == owner, fitted, fit_row)

    def take(p, first, local, sums):
        def add(src, ref, sums):
            tile = ref[src, p].astype(F32)
            row = (first + src) * aux_local + local
            return tuple(
                total + tile * integral[c, row].astype(F32) for c, total in enumerate(sums)
            )

        def arrive(k, sums):
            src = xor(spot, k)
            tiles(p, src, src).wait_recv()
            return add(src, arrived, sums)

        return lax.fori_loop(1, half, arrive, add(spot, chosen, sums))

    fit_row = jnp.zeros(fits.shape[1:], F32)
    for p in range(aux_local):
        fit_row = density(b_ref[p], p, me * aux_local + p, fit_row)

    fa = atom_ref[...]
    atom_table = (iota((128, 256), 0) == fa).astype(F32).T.astype(BF16)
    spread = (iota((256, 256), 0) // TILE == iota((256, 256), 1) % TILE).astype(BF16)
    own = jnp.zeros((depth, 1), jnp.int32)
    wide_list = list_ref[...]
    own_lane = iota((depth, slots), 1) == me * depth + iota((depth, slots), 0)
    own = jnp.sum(jnp.where(own_lane, wide_list.astype(F32), 0.0), axis=1, keepdims=True)
    own = own.astype(jnp.int32)
    live = iota((depth, 256), 0) < count_ref[me]
    row_mask = live & (own // TILE == iota((depth, 256), 1) // TILE)

    for load in loads:
        load.wait()

    sums = tuple(jnp.zeros((depth, 256), F32) for _ in range(3))
    order = [(d, q) for q in range(share) for d in range(groups)]
    for place, (d, q) in enumerate(order):
        source = lax.rem(group + groups - d, groups)
        if d == 0:
            far(q).wait_recv()
            for e in range(1, groups):
                near(e, q, group).start()
        else:
            near(d, q, source).wait_recv()
        p = source * share + q
        fit_row = density(
            foreign[p], aux_local + p, counterpart * aux_local + p, fit_row
        )
        if place == aux_local - 2:
            for own_p in range(aux_local):
                sums = take(own_p, base, own_p, sums)
    fits[spot] = fit_row

    def send_fit(k, c):
        fit_to(xor(spot, half - k), spot).start()
        return c

    lax.fori_loop(1, half, send_fit, 0)
    for d, q in order:
        source = lax.rem(group + groups - d, groups)
        p = source * share + q
        sums = take(aux_local + p, other_base, p, sums)

    def arrive_fit(k, total):
        src = xor(spot, k)
        fit_to(src, src).wait_recv()
        return total + fits[src]

    all_fits = lax.fori_loop(1, half, arrive_fit, fit_row)

    rows = iota((aux_local, all_fits.shape[1]), 0)
    lanes = iota((aux_local, all_fits.shape[1]), 1)
    fit_column = jnp.sum(
        jnp.where(lanes == me * aux_local + rows, fit_row, 0.0), axis=1, keepdims=True
    )
    width = metric_ref.shape[2]
    mine = jnp.zeros((1, 128), F32)
    weighted = []
    for c in range(3):
        coupling = jnp.sum(metric_ref[c].astype(F32) * all_fits[:, :width], axis=1, keepdims=True)
        weighted.append(coupling * fit_column)
    for p in range(aux_local):
        for c in range(3):
            hit = iota((1, 128), 1) == center_ref[p] + c * NATOM
            mine = mine - jnp.where(hit, weighted[c][p : p + 1], 0.0)

    by_function = select_dot(jnp.concatenate(sums, axis=0), spread)
    by_function = [
        jnp.sum(
            jnp.where(row_mask, by_function[c * depth : (c + 1) * depth], 0.0),
            axis=0,
            keepdims=True,
        )
        for c in range(3)
    ]
    by_function = jnp.concatenate(by_function + [jnp.zeros((5, 256), F32)], axis=0)
    by_atom = 2.0 * select_dot(by_function, atom_table)
    lane = iota((1, 128), 1)
    for c in range(3):
        row = by_atom[c : c + 1]
        if c:
            row = pltpu.roll(by_atom, c * NATOM, 1)[c : c + 1]
        mine = mine + jnp.where(lane // NATOM == c, row, 0.0)
    parts[me] = mine

    def send_part(k, c):
        part_to(xor(me, n - k), me).start()
        return c

    lax.fori_loop(1, n, send_part, 0)

    def drain(k, c):
        peer = xor(spot, k)
        fit_to(peer, spot).wait_send()
        for p in range(2 * aux_local):
            tiles(p, peer, spot).wait_send()
        return c

    lax.fori_loop(1, half, drain, 0)
    for q in range(share):
        far(q).wait_send()
        for e in range(1, groups):
            near(e, q, group).wait_send()

    def take_part(k, total):
        src = xor(me, k)
        part_to(src, src).wait_recv()
        return total

    lax.fori_loop(1, n, take_part, 0)
    total = jnp.sum(parts[...], axis=0)
    for c in range(3):
        out_ref[c : c + 1] = total[:, c * NATOM : (c + 1) * NATOM]

    def drain_parts(k, c):
        part_to(xor(me, k), me).wait_send()
        return c

    lax.fori_loop(1, n, drain_parts, 0)


def on_device(
    n,
    groups,
    three_index,
    relaxed,
    plus_amplitude,
    minus_amplitude,
    ground,
    integral_grad,
    metric_grad,
    function_atom,
    aux_center,
    block_list,
    block_count,
):
    aux_local = three_index.shape[0]
    aux_total, depth, width = integral_grad.shape[1:]
    fit_lanes = -(-aux_total // 128) * 128
    half = n // 2
    share = aux_local // groups
    vmem = pl.BlockSpec(memory_space=pltpu.VMEM)
    smem = pl.BlockSpec(memory_space=pltpu.SMEM)
    anywhere = pl.BlockSpec(memory_space=pl.ANY)
    dma = pltpu.SemaphoreType.DMA
    return pl.pallas_call(
        functools.partial(gradient_kernel, n, groups),
        out_shape=jax.ShapeDtypeStruct((3, NATOM), F32),
        in_specs=[smem, smem] + [vmem] * 8 + [anywhere],
        out_specs=vmem,
        scratch_shapes=[
            pltpu.VMEM((3, aux_total, depth, width), BF16),
            pltpu.VMEM(three_index.shape, BF16),
            pltpu.VMEM((half, 2 * aux_local, depth, width), BF16),
            pltpu.VMEM((half, 2 * aux_local, depth, width), BF16),
            pltpu.VMEM((half, 1, fit_lanes), F32),
            pltpu.VMEM((n, 1, 128), F32),
            dma((3,)),
            dma((share,)),
            dma((share,)),
            dma((max(groups - 1, 1), share)),
            dma((max(groups - 1, 1), share)),
            dma((2 * aux_local, half)),
            dma((2 * aux_local, half)),
            dma((half,)),
            dma((half,)),
            dma((n,)),
            dma((n,)),
        ],
        compiler_params=pltpu.CompilerParams(collective_id=0, has_side_effects=True),
        name="gradient",
    )(
        block_count,
        aux_center,
        three_index,
        relaxed,
        plus_amplitude,
        minus_amplitude,
        ground,
        metric_grad,
        block_list.reshape(1, -1),
        function_atom.reshape(1, -1),
        integral_grad,
    )


def solution(mesh):
    in_specs = (
        P("aux", None, None),
        P("grp", None),
        P("grp", None),
        P("grp", None),
        P(),
        P(None, None, "aux", None),
        P(None, "aux", None),
        P(),
        P("aux"),
        P(),
        P(),
    )
    out_specs = P(None, "grp")
    return jax.shard_map(
        functools.partial(on_device, mesh.shape["aux"], mesh.shape["grp"]),
        mesh=mesh,
        in_specs=in_specs,
        out_specs=out_specs,
        check_vma=False,
    )
```

time: 49.9 us -> 41.6 us (0.83)
  Pallas kernels: 46.9 us -> 40.2 us
  local copies, waits for them, and re-layouts: 2.79 us -> 1.26 us
    pallas_call x2 -> x1, Pallas kernels: 46.9 us -> 40.2 us  [on_device(): pl.pallas_call(functools.partial(gradient_kernel, n, groups), out_shape=j...]
    reshape x1 -> x0, local copies, waits for them, and re-layouts: 1.54 us -> none  [on_device(): column = block_list.reshape(slots, 1)]
where the time goes in v2:
time: 41.6 us; the launch traced here: 41.5 us
  Pallas kernels  40.2 us (97%)
  local copies, waits for them, and re-layouts  1.26 us (3%)
    pallas_call x1, Pallas kernels, on_device(): pl.pallas_call(functools.partial(gradient_kernel, n, groups), out_shape=j...  40.2 us
    unnamed x1, local copies, waits for them, and re-layouts  1.26 us

profile of v2, /device:TPU:0, one launch (start us, length us, event | category | flops | bytes accessed | tf_op | source)
XLA Modules:
  0.0 41.5 jit_solution(3404198220353803139)
XLA Ops:
  0.0 40.2 %gradient.1 = f32[3,32]{1,0:T(4,128)} custom-call(s32[16]{0:T(128)} %count_ref.1, s32[4]{0:T(128)} %center_ref.1, bf16[4,256,256]{2,1,0:T(8,128)(2,1)} %b_ref.1, bf16[256,256]{1,0:T(8,128)(2,1)} %relaxed_ref.1, bf16[256,256]{1,0:T(8,128)(2,1)} %plus_ref.1, bf16[256,256]{1,0:T(8,128)(2,1)} %minus_ref.1, bf16[256,256]{1,0:T(8,128)(2,1)} %ground_ref.1, ...), custom_call_target="tpu_custom_call" | custom-call | tf_op jit(solution)/shard_map/gradient/pallas_call | solution.py:395
  40.2 1.3 %copy.13 = f32[3,32]{1,0:T(4,128)} copy(f32[3,32]{1,0:T(4,128)} %gradient.1) | data formatting | bytes 768

commit v3 on v2

--- a/solution.py
+++ b/solution.py
@@ -64,17 +64,19 @@
     groups,
     count_ref,
     center_ref,
-    b_ref,
+    metric_ref,
+    list_ref,
+    atom_ref,
+    slab_ref,
     relaxed_ref,
     plus_ref,
     minus_ref,
     ground_ref,
-    metric_ref,
-    list_ref,
-    atom_ref,
     integral_ref,
     out_ref,
     integral,
+    b_ref,
+    mats,
     foreign,
     chosen,
     arrived,
@@ -95,6 +97,7 @@
     me = lax.axis_index("aux")
     group = lax.axis_index("grp")
     half = n // 2
+    piece = slab_ref.shape[1] // 2
     depth = integral.shape[2]
     aux_local = b_ref.shape[0]
     share = aux_local // groups
@@ -105,49 +108,60 @@
     other_base = (1 - side) * half
     counterpart = other_base + spot
 
-    loads = [
-        pltpu.make_async_copy(integral_ref.at[c], integral.at[c], load_sems.at[c]) for c in range(3)
-    ]
-    for load in loads:
-        load.start()
-
     barrier = pltpu.get_barrier_semaphore()
 
+    def flips(a):
+        bits = [1 << i for i in range(n.bit_length() - 1)]
+        return [(bit, bit * (1 - 2 * ((a // bit) % 2))) for bit in bits]
+
+    me_flips, spot_flips = flips(me), flips(spot)
+
     def xor(a, k):
-        value, bit = me - me, 1
-        while bit < n:
-            value = value + ((a // bit) % 2 + (k // bit) % 2) % 2 * bit
-            bit *= 2
+        value = a
+        for bit, change in me_flips if a is me else spot_flips:
+            if isinstance(k, int):
+                value = value + change if k & bit else value
+            else:
+                value = value + change * ((k // bit) % 2)
         return value
+
+    def loop(first, last, body, carry):
+        if n > 16:
+            return lax.fori_loop(first, last, body, carry)
+        for k in range(first, last):
+            carry = body(k, carry)
+        return carry
 
     def greet(k, c):
         pl.semaphore_signal(barrier, inc=1, device_id={"aux": xor(me, k)}, device_id_type=MESH)
         return c
 
-    lax.fori_loop(1, n, greet, 0)
+    loop(1, n, greet, 0)
     for d in range(1, groups):
         pl.semaphore_signal(
             barrier, inc=1, device_id={"grp": lax.rem(group + d, groups)}, device_id_type=MESH
         )
 
-    def far(q):
+    def far(q, h):
         p = group * share + q
+        rows = pl.ds(h * piece, piece)
         return pltpu.make_async_remote_copy(
-            src_ref=b_ref.at[p],
-            dst_ref=foreign.at[p],
-            send_sem=far_send.at[q],
-            recv_sem=far_recv.at[q],
+            src_ref=slab_ref.at[p, rows],
+            dst_ref=foreign.at[p, rows],
+            send_sem=far_send.at[q, h],
+            recv_sem=far_recv.at[q, h],
             device_id={"aux": counterpart},
             device_id_type=MESH,
         )
 
-    def near(d, q, source):
+    def near(d, q, h, source):
         p = source * share + q
+        rows = pl.ds(h * piece, piece)
         return pltpu.make_async_remote_copy(
-            src_ref=foreign.at[p],
-            dst_ref=foreign.at[p],
-            send_sem=near_send.at[d - 1, q],
-            recv_sem=near_recv.at[d - 1, q],
+            src_ref=foreign.at[p, rows],
+            dst_ref=foreign.at[p, rows],
+            send_sem=near_send.at[d - 1, q, h],
+            recv_sem=near_recv.at[d - 1, q, h],
             device_id={"grp": lax.rem(group + d, groups)},
             device_id_type=MESH,
         )
@@ -182,42 +196,49 @@
             device_id_type=MESH,
         )
 
+    loads = [
+        pltpu.make_async_copy(ref, mats.at[i], load_sems.at[i])
+        for i, ref in enumerate((relaxed_ref, plus_ref, minus_ref, ground_ref))
+    ]
+    loads.append(pltpu.make_async_copy(slab_ref, b_ref, load_sems.at[4]))
+    late = [
+        pltpu.make_async_copy(integral_ref.at[c], integral.at[c], load_sems.at[5 + c])
+        for c in range(3)
+    ]
+    for load in loads + late:
+        load.start()
     pl.semaphore_wait(barrier, n - 1 + groups - 1)
     for q in range(share):
-        far(q).start()
-
-    relaxed = relaxed_ref[...]
-    a = iota((256, 256), 0)
-    b = iota((256, 256), 1)
-    perm = ((a % TILE) * TILE + a // TILE == b).astype(BF16)
-    plus = dot(perm, plus_ref[...]).astype(BF16)
-    minus = dot(perm, minus_ref[...]).astype(BF16)
-    ground = dot(perm, ground_ref[...]).astype(BF16)
-    relaxed_cols = dot(relaxed, perm, 1, 1).astype(BF16)
-    relaxed_turned = dot(perm, relaxed, 1, 1).astype(BF16)
-    relaxed_both = dot(perm, relaxed_cols)
+        for h in range(2):
+            far(q, h).start()
+    for load in loads:
+        load.wait()
+
+    relaxed = mats[0]
+    stacked = mats[1:4].reshape(3 * 256, 256)
     relaxed_wide = relaxed.astype(F32)
+    turned = relaxed_wide.T.astype(BF16)
+    partners = jnp.concatenate(
+        [mats[1].astype(F32).T, -(mats[2].astype(F32).T), relaxed_wide], axis=0
+    ).astype(BF16)
     half_slots = slots // 2
     listed = list_ref[...]
     listed = jnp.where(side == 0, listed[:, :half_slots], listed[:, half_slots:])
     picked = (listed == iota((256, half_slots), 0)).astype(F32).T.astype(BF16)
     fit_lane = iota(fits.shape[1:], 1)
 
+
     def density(slab, p, owner, fit_row):
         fitted = jnp.sum(slab.astype(F32) * relaxed_wide, axis=0, keepdims=True)
         fitted = jnp.sum(fitted, axis=1, keepdims=True)
-        plus_half = dot(plus, slab).astype(BF16)
-        minus_half = dot(minus, slab).astype(BF16)
-        ground_half = dot(ground, slab).astype(BF16)
+        halves = dot(stacked, slab).astype(BF16)
+        ground_half = halves[512:]
+        joined = jnp.concatenate([halves[:256], halves[256:512], ground_half], axis=1)
         triple = (
-            fitted * relaxed_both
-            + dot(plus_half, plus, 1, 1)
-            - dot(minus_half, minus, 1, 1)
-            + dot(ground_half, relaxed_cols)
-            + dot(relaxed_turned, ground_half, 1, 1)
+            fitted * relaxed_wide + dot(joined, partners) + dot(turned, ground_half, 1, 1)
         )
         blocked = swap_tiles(triple.astype(BF16).astype(F32)).astype(BF16)
-        tile_rows = dot(picked, blocked, 1, 1)
+        tile_rows = dot(picked, blocked)
         chosen[:, p] = tile_rows.reshape(half, depth, 256).astype(BF16)
 
         def send(k, c):
@@ -225,7 +246,7 @@
             tiles(p, peer, spot).start()
             return c
 
-        lax.fori_loop(1, half, send, 0)
+        loop(1, half, send, 0)
         return jnp.where(fit_lane == owner, fitted, fit_row)
 
     def take(p, first, local, sums):
@@ -241,7 +262,7 @@
             tiles(p, src, src).wait_recv()
             return add(src, arrived, sums)
 
-        return lax.fori_loop(1, half, arrive, add(spot, chosen, sums))
+        return loop(1, half, arrive, add(spot, chosen, sums))
 
     fit_row = jnp.zeros(fits.shape[1:], F32)
     for p in range(aux_local):
@@ -258,24 +279,25 @@
     live = iota((depth, 256), 0) < count_ref[me]
     row_mask = live & (own // TILE == iota((depth, 256), 1) // TILE)
 
-    for load in loads:
+    for load in late:
         load.wait()
 
     sums = tuple(jnp.zeros((depth, 256), F32) for _ in range(3))
     order = [(d, q) for q in range(share) for d in range(groups)]
-    for place, (d, q) in enumerate(order):
+    for d, q in order:
         source = lax.rem(group + groups - d, groups)
-        if d == 0:
-            far(q).wait_recv()
-            for e in range(1, groups):
-                near(e, q, group).start()
-        else:
-            near(d, q, source).wait_recv()
+        for h in range(2):
+            if d == 0:
+                far(q, h).wait_recv()
+                for e in range(1, groups):
+                    near(e, q, h, group).start()
+            else:
+                near(d, q, h, source).wait_recv()
         p = source * share + q
         fit_row = density(
             foreign[p], aux_local + p, counterpart * aux_local + p, fit_row
         )
-        if place == aux_local - 2:
+        if (d, q) == (0, share - 1):
             for own_p in range(aux_local):
                 sums = take(own_p, base, own_p, sums)
     fits[spot] = fit_row
@@ -284,7 +306,7 @@
         fit_to(xor(spot, half - k), spot).start()
         return c
 
-    lax.fori_loop(1, half, send_fit, 0)
+    loop(1, half, send_fit, 0)
     for d, q in order:
         source = lax.rem(group + groups - d, groups)
         p = source * share + q
@@ -295,7 +317,7 @@
         fit_to(src, src).wait_recv()
         return total + fits[src]
 
-    all_fits = lax.fori_loop(1, half, arrive_fit, fit_row)
+    all_fits = loop(1, half, arrive_fit, fit_row)
 
     rows = iota((aux_local, all_fits.shape[1]), 0)
     lanes = iota((aux_local, all_fits.shape[1]), 1)
@@ -336,7 +358,7 @@
         part_to(xor(me, n - k), me).start()
         return c
 
-    lax.fori_loop(1, n, send_part, 0)
+    loop(1, n, send_part, 0)
 
     def drain(k, c):
         peer = xor(spot, k)
@@ -345,27 +367,29 @@
             tiles(p, peer, spot).wait_send()
         return c
 
-    lax.fori_loop(1, half, drain, 0)
+    loop(1, half, drain, 0)
     for q in range(share):
-        far(q).wait_send()
-        for e in range(1, groups):
-            near(e, q, group).wait_send()
+        for h in range(2):
+            far(q, h).wait_send()
+            for e in range(1, groups):
+                near(e, q, h, group).wait_send()
 
     def take_part(k, total):
         src = xor(me, k)
         part_to(src, src).wait_recv()
         return total
 
-    lax.fori_loop(1, n, take_part, 0)
+    loop(1, n, take_part, 0)
     total = jnp.sum(parts[...], axis=0)
     for c in range(3):
-        out_ref[c : c + 1] = total[:, c * NATOM : (c + 1) * NATOM]
+        row = pltpu.roll(jnp.broadcast_to(total, (8, 128)), 128 - c * NATOM, 1) if c else total
+        out_ref[c : c + 1] = row[:1]
 
     def drain_parts(k, c):
         part_to(xor(me, k), me).wait_send()
         return c
 
-    lax.fori_loop(1, n, drain_parts, 0)
+    loop(1, n, drain_parts, 0)
 
 
 def on_device(
@@ -392,23 +416,25 @@
     smem = pl.BlockSpec(memory_space=pltpu.SMEM)
     anywhere = pl.BlockSpec(memory_space=pl.ANY)
     dma = pltpu.SemaphoreType.DMA
-    return pl.pallas_call(
+    out = pl.pallas_call(
         functools.partial(gradient_kernel, n, groups),
-        out_shape=jax.ShapeDtypeStruct((3, NATOM), F32),
-        in_specs=[smem, smem] + [vmem] * 8 + [anywhere],
+        out_shape=jax.ShapeDtypeStruct((3, 128), F32),
+        in_specs=[smem, smem] + [vmem] * 3 + [anywhere] * 6,
         out_specs=vmem,
         scratch_shapes=[
             pltpu.VMEM((3, aux_total, depth, width), BF16),
+            pltpu.VMEM(three_index.shape, BF16),
+            pltpu.VMEM((4, *relaxed.shape), BF16),
             pltpu.VMEM(three_index.shape, BF16),
             pltpu.VMEM((half, 2 * aux_local, depth, width), BF16),
             pltpu.VMEM((half, 2 * aux_local, depth, width), BF16),
             pltpu.VMEM((half, 1, fit_lanes), F32),
             pltpu.VMEM((n, 1, 128), F32),
-            dma((3,)),
-            dma((share,)),
-            dma((share,)),
-            dma((max(groups - 1, 1), share)),
-            dma((max(groups - 1, 1), share)),
+            dma((8,)),
+            dma((share, 2)),
+            dma((share, 2)),
+            dma((max(groups - 1, 1), share, 2)),
+            dma((max(groups - 1, 1), share, 2)),
             dma((2 * aux_local, half)),
             dma((2 * aux_local, half)),
             dma((half,)),
@@ -421,16 +447,17 @@
     )(
         block_count,
         aux_center,
+        metric_grad,
+        block_list.reshape(1, -1),
+        function_atom.reshape(1, -1),
         three_index,
         relaxed,
         plus_amplitude,
         minus_amplitude,
         ground,
-        metric_grad,
-        block_list.reshape(1, -1),
-        function_atom.reshape(1, -1),
         integral_grad,
     )
+    return out[:, :NATOM]
 
 
 def solution(mesh):

time: 41.6 us -> 39.2 us (0.942)
  Pallas kernels: 40.2 us -> 37.8 us
    pallas_call x1, Pallas kernels: 40.2 us -> 37.8 us  [on_device(): pl.pallas_call(functools.partial(gradient_kernel, n, groups), out_shape=j...]
where the time goes in v3:
time: 39.2 us; the launch traced here: 39 us
  Pallas kernels  37.8 us (96%)
  local copies, waits for them, and re-layouts  1.26 us (3%)
    pallas_call x1, Pallas kernels, on_device(): pl.pallas_call(functools.partial(gradient_kernel, n, groups), out_shape=j...  37.8 us
    unnamed x1, local copies, waits for them, and re-layouts  1.26 us

profile of v3, /device:TPU:0, one launch (start us, length us, event | category | flops | bytes accessed | tf_op | source)
XLA Modules:
  0.0 39.0 jit_solution(12741928625340237811)
XLA Ops:
  0.0 37.8 %gradient.1 = f32[3,128]{1,0:T(4,128)} custom-call(s32[16]{0:T(128)} %count_ref.1, s32[4]{0:T(128)} %center_ref.1, bf16[3,4,64]{2,1,0:T(4,128)(2,1)} %metric_ref.1, s32[1,512]{1,0:T(1,128)} %bitcast.4, s32[1,256]{1,0:T(1,128)} %bitcast.5, bf16[4,256,256]{2,1,0:T(8,128)(2,1)} %slab_ref.1, bf16[256,256]{1,0:T(8,128)(2,1)} %relaxed_ref.1, ...), custom_call_target="tpu_custom_call" | custom-call | tf_op jit(solution)/shard_map/gradient/pallas_call | solution.py:419
  37.8 1.3 %copy.13 = f32[3,32]{1,0:T(4,128)} copy(f32[3,32]{1,0:T(4,128)} %bitcast.3) | data formatting | bytes 768

commit v4 on v3

--- a/solution.py
+++ b/solution.py
@@ -264,8 +264,15 @@
 
         return loop(1, half, arrive, add(spot, chosen, sums))
 
+    def forward(q, h):
+        far(q, h).wait_recv()
+        for e in range(1, groups):
+            near(e, q, h, group).start()
+
     fit_row = jnp.zeros(fits.shape[1:], F32)
     for p in range(aux_local):
+        if p == aux_local - 1:
+            forward(0, 0)
         fit_row = density(b_ref[p], p, me * aux_local + p, fit_row)
 
     fa = atom_ref[...]
@@ -287,12 +294,13 @@
     for d, q in order:
         source = lax.rem(group + groups - d, groups)
         for h in range(2):
-            if d == 0:
-                far(q, h).wait_recv()
-                for e in range(1, groups):
-                    near(e, q, h, group).start()
-            else:
+            if d:
                 near(d, q, h, source).wait_recv()
+            elif q == 0 and h == 1:
+                forward(q, h)
+        if d == groups - 1 and q + 1 < share:
+            for h in range(2):
+                forward(q + 1, h)
         p = source * share + q
         fit_row = density(
             foreign[p], aux_local + p, counterpart * aux_local + p, fit_row

time: 39.2 us -> 38.1 us (0.972)
  Pallas kernels: 37.8 us -> 36.7 us
    pallas_call x1, Pallas kernels: 37.8 us -> 36.7 us  [on_device(): pl.pallas_call(functools.partial(gradient_kernel, n, groups), out_shape=j...]
where the time goes in v4:
time: 38.1 us; the launch traced here: 37.9 us
  Pallas kernels  36.7 us (96%)
  local copies, waits for them, and re-layouts  1.26 us (3%)
    pallas_call x1, Pallas kernels, on_device(): pl.pallas_call(functools.partial(gradient_kernel, n, groups), out_shape=j...  36.7 us
    unnamed x1, local copies, waits for them, and re-layouts  1.26 us

profile of v4, /device:TPU:0, one launch (start us, length us, event | category | flops | bytes accessed | tf_op | source)
XLA Modules:
  0.0 37.9 jit_solution(12170434269568348852)
XLA Ops:
  0.0 36.7 %gradient.1 = f32[3,128]{1,0:T(4,128)} custom-call(s32[16]{0:T(128)} %count_ref.1, s32[4]{0:T(128)} %center_ref.1, bf16[3,4,64]{2,1,0:T(4,128)(2,1)} %metric_ref.1, s32[1,512]{1,0:T(1,128)} %bitcast.4, s32[1,256]{1,0:T(1,128)} %bitcast.5, bf16[4,256,256]{2,1,0:T(8,128)(2,1)} %slab_ref.1, bf16[256,256]{1,0:T(8,128)(2,1)} %relaxed_ref.1, ...), custom_call_target="tpu_custom_call" | custom-call | tf_op jit(solution)/shard_map/gradient/pallas_call | solution.py:427
  36.7 1.3 %copy.13 = f32[3,32]{1,0:T(4,128)} copy(f32[3,32]{1,0:T(4,128)} %bitcast.3) | data formatting | bytes 768
